TPU v7x, 32 devices: a whole 2x2x4 slice. The times are simulated.
32 devices in a mesh: grp: 2 (over y), comp: 4 (over z), space: 4 (over x, core).
Axes of the slice: x: 2, y: 2, z: 4, core: 2. Of those that a mesh axis runs over, the one named last changes fastest.
Arguments:
- spectrum: float32 [2304, 4096], P('comp', ('grp', 'space')), parts along dimension 1, may hold values from -6 to 6
- wave_speed: float32 [36], replicated, may hold values from 0.25 to 2
- current_east: float32 [4096], P(('grp', 'space')), parts along dimension 0, may hold values from -3 to 3
- current_north: float32 [4096], P(('grp', 'space')), parts along dimension 0, may hold values from -3 to 3
- substeps: int32 [2304], replicated, may hold values from 1 to 4, as said below
- neighbours: int32 [4, 4096], P(None, ('grp', 'space')), parts along dimension 1, may hold values from 0 to 767, as said below
- blocks: bfloat16 [64, 64, 64], replicated, may hold values from -0.75 to 0.75
- quad_index: int32 [4, 64], replicated, may hold values from 0 to 35
- strength: float32 [64], replicated, may hold values from -1 to 1
Outputs:
- spectrum_out: float32 [2304, 4096], P('comp', ('grp', 'space')), parts along dimension 1
There are 2 independent parts, one for each index of `grp`. A program takes and returns all parts, laid end to end along the dimension named above; an argument that names none is the same for every part. Nothing has to cross between parts.
Inputs may be any that keep to these rules, and one draw needn't show every extreme that they name: `substeps`: component 0 takes 4. `neighbours`: the entry of row r for the slab's point q (counted within its slab) is q + 128 + o, with -128 <= o <= -1 for rows 0 and 2 and 1 <= o <= 128 for rows 1 and 3.
All inputs are finite; a program needn't handle non-finite values.
Results may differ from a plain program's by a relative error of at most 0.00031.
Values sent between devices are 32-bit elements; how exact they have to be, the bound alone decides.
A program may use at most 64 MiB of HBM per device.

v0:
```python
import math

import jax
import jax.numpy as jnp
from jax import lax
from jax.sharding import PartitionSpec as P

NF = 36
ND = 64
SUB = 4
HALO = 128


courant_scale = 0.4
courant_limit = 0.45
source_step = 0.1


def padded(cells, sides, width):
    for axis, dim in sides:
        count = lax.axis_size(axis)
        ends = count - 1
        head = lax.slice_in_dim(cells, 0, width, axis=dim)
        tail = lax.slice_in_dim(cells, cells.shape[dim] - width, cells.shape[dim], axis=dim)
        cells = jnp.concatenate(
            [
                lax.ppermute(tail, axis, [(i, (i + 1) % count) for i in range(ends)]),
                cells,
                lax.ppermute(head, axis, [((i + 1) % count, i) for i in range(ends)]),
            ],
            axis=dim,
        )
    return cells


def upwind(spectra, first_comp, substeps, wave_speed, current_east, current_north, neighbours):
    row_count = spectra.shape[0]
    components = first_comp + jnp.arange(row_count, dtype=jnp.int32)
    frequency = components // ND
    angles = ((components % ND).astype(jnp.float32) + 0.5) * (2.0 * math.pi / ND)
    matches = frequency[:, None] == jnp.arange(NF, dtype=jnp.int32)[None, :]
    group_speed = jnp.sum(jnp.where(matches, wave_speed[None, :], 0.0), axis=1)
    counts = lax.dynamic_slice_in_dim(substeps, first_comp, row_count)
    divisor = counts.astype(jnp.float32)[:, None]
    along_x = jnp.clip(
        ((group_speed * jnp.cos(angles))[:, None] + current_east[None, :])
        * courant_scale
        / divisor,
        -courant_limit,
        courant_limit,
    )
    along_y = jnp.clip(
        ((group_speed * jnp.sin(angles))[:, None] + current_north[None, :])
        * courant_scale
        / divisor,
        -courant_limit,
        courant_limit,
    )
    pos_x = jnp.maximum(along_x, 0.0)
    neg_x = jnp.minimum(along_x, 0.0)
    pos_y = jnp.maximum(along_y, 0.0)
    neg_y = jnp.minimum(along_y, 0.0)

    def sweep_once(repeat, values):
        extended = padded(values, (("space", 1),), HALO)
        west_value = jnp.take(extended, neighbours[0], axis=1)
        east_value = jnp.take(extended, neighbours[1], axis=1)
        south_value = jnp.take(extended, neighbours[2], axis=1)
        north_value = jnp.take(extended, neighbours[3], axis=1)
        updated = (
            values
            - pos_x * (values - west_value)
            - neg_x * (east_value - values)
            - pos_y * (values - south_value)
            - neg_y * (north_value - values)
        )
        return jnp.where(repeat < counts[:, None], updated, values)

    return lax.fori_loop(0, SUB, sweep_once, spectra)


def to_points(spectra, peers):
    row_count, columns = spectra.shape
    pieces = spectra.reshape(row_count, peers, columns // peers)
    arrived = lax.all_to_all(pieces, "comp", split_axis=1, concat_axis=0, tiled=True)
    return arrived.reshape(row_count * peers, columns // peers)


def to_components(points, peers):
    total_rows, columns = points.shape
    pieces = points.reshape(total_rows, 1, columns)
    arrived = lax.all_to_all(pieces, "comp", split_axis=0, concat_axis=1, tiled=True)
    return arrived.reshape(total_rows // peers, peers * columns)


def source_term(spectra, blocks, quad_index, strength):
    columns = spectra.shape[1]
    block_total = blocks.shape[0]
    group_size = math.gcd(block_total, 32)
    group_count = block_total // group_size
    spectra_grid = spectra.reshape(NF, ND, columns)
    rounded = spectra_grid.astype(jnp.bfloat16)
    block_sets = blocks.reshape(group_count, group_size, ND, ND)
    quad_sets = quad_index.reshape(4, group_count, group_size).transpose(1, 0, 2)
    weight_sets = strength.reshape(group_count, group_size)

    def accumulate(total, members):
        block_set, quad_set, weight_set = members
        first_rows = rounded[quad_set[0]]
        second = rounded[quad_set[1]]
        third_rows = spectra_grid[quad_set[2]]
        left_term = jnp.einsum(
            "jde,jep->jdp", block_set, first_rows, preferred_element_type=jnp.float32
        )
        right_term = jnp.einsum(
            "jed,jep->jdp", block_set, second, preferred_element_type=jnp.float32
        )
        product = (left_term * right_term * third_rows).astype(jnp.bfloat16)
        part_term = jnp.einsum(
            "jde,jep->jdp", block_set, product, preferred_element_type=jnp.float32
        )
        total = total.at[quad_set[3]].add(weight_set[:, None, None] * part_term)
        return (total, None)

    total, unused = lax.scan(
        accumulate, jnp.zeros((NF, ND, columns), jnp.float32), (block_sets, quad_sets, weight_sets)
    )
    return (spectra_grid + source_step * total).reshape(NF * ND, columns)


def shards(
    spectrum,
    wave_speed,
    current_east,
    current_north,
    substeps,
    neighbours,
    blocks,
    quad_index,
    strength,
):
    peers = lax.axis_size("comp")
    row_count = spectrum.shape[0]
    own_index = lax.axis_index("comp")
    first_comp = own_index * row_count
    spectra = spectrum
    spectra = upwind(
        spectra, first_comp, substeps, wave_speed, current_east, current_north, neighbours
    )
    points = source_term(to_points(spectra, peers), blocks, quad_index, strength)
    spectra = to_components(points, peers)
    return spectra


def solution(mesh):
    in_specs = (
        P("comp", ("grp", "space")),
        P(),
        P(("grp", "space")),
        P(("grp", "space")),
        P(),
        P(None, ("grp", "space")),
        P(),
        P(),
        P(),
    )
    out_specs = P("comp", ("grp", "space"))
    return jax.shard_map(shards, mesh=mesh, in_specs=in_specs, out_specs=out_specs, check_vma=False)
```

profile of v0, /device:TPU:0, one launch (start us, length us, event | category | flops | bytes accessed | tf_op | source)
XLA Modules:
  0.0 204.3 jit_solution(14900403641817318746)
XLA Ops:
  0.8 1.7 copy.31
  3.3 103.0 %while.26 = (s32[]{:T(128)}, f32[576,512]{0,1:T(8,128)S(1)}, s32[576]{0:T(1024)S(1)}, s32[4,512]{1,0:T(4,128)S(1)}, f32[512]{0:T(512)S(1)}, /*index=5*/f32[576]{...) while((s32[]{:T(128)}, f32[576,512]{0,1:T(8,128)S(1)}, ...), condition=%wide.region_2.4_spmd.clone.clone, body=%wide.region_1.3_spmd.clone.clone.sunk | while | flops 8575554 | bytes 24013112 | solution.py:79
  4.1 3.1 %collective-permute-start = (f32[576,128]{0,1:T(8,128)S(1)}, f32[576,128]{0,1:T(8,128)}, u32[]{:S(2)}, u32[]{:S(2)}) collective-permute-start(f32[576,128]{0,1:T(8,128)S(1)} %get-tuple-element.533), channel_id=1, source_target_pairs={{0,1},{1,2},{2,3},{4,5},{5,6},{6,7},{8,9},{9,10},{10,11},{12,13},{... | collective-permute-start | bytes 884744 | tf_op jit(solution)/shard_map/while/body/eval_jaxpr/ppermute | solution.py:27
  7.2 1.3 collective-permute-start.1
  9.7 2.7 %collective-permute-done.1 = f32[576,128]{0,1:T(8,128)} collective-permute-done((f32[576,128]{0,1:T(8,128)}, f32[576,128]{0,1:T(8,128)}, u32[]{:S(2)}, u32[]{:S(2)}) %collective-permute-start.1) | collective-permute-done | bytes 294944 | tf_op jit(solution)/shard_map/while/body/eval_jaxpr/ppermute | solution.py:29
  13.5 2.6 %gather_fusion.4 = f32[512,576]{1,0:T(8,128)} fusion(f32[576,768]{0,1:T(8,128)S(1)} %constant_dynamic-update-slice_fusion.8, s32[1024]{0:T(1024)S(1)} %get-tuple-element.538), kind=kCustom, calls=%fused_computation.5.clone.clone.1 | custom fusion | bytes 2361344 | tf_op jit(solution)/shard_map/while/body/eval_jaxpr/jit(_take)/gather | solution.py:68
  16.0 2.5 %gather_fusion.5 = f32[512,576]{1,0:T(8,128)} fusion(f32[576,768]{0,1:T(8,128)S(1)} %constant_dynamic-update-slice_fusion.8, s32[1024]{0:T(1024)S(1)} %get-tuple-element.541), kind=kCustom, calls=%fused_computation.4.clone.clone.1 | custom fusion | bytes 2361344 | tf_op jit(solution)/shard_map/while/body/eval_jaxpr/jit(_take)/gather | solution.py:67
  18.6 2.6 %gather_fusion.6 = f32[512,576]{1,0:T(8,128)} fusion(f32[576,768]{0,1:T(8,128)S(1)} %constant_dynamic-update-slice_fusion.8, s32[1024]{0:T(1024)S(1)} %get-tuple-element.542), kind=kCustom, calls=%fused_computation.clone.clone.1 | custom fusion | bytes 2361344 | tf_op jit(solution)/shard_map/while/body/eval_jaxpr/jit(_take)/gather | solution.py:66
  21.1 2.6 %gather_fusion.3 = f32[512,576]{1,0:T(8,128)} fusion(f32[576,768]{0,1:T(8,128)S(1)} %constant_dynamic-update-slice_fusion.8, s32[1024]{0:T(1024)S(1)} %get-tuple-element.537), kind=kCustom, calls=%fused_computation.6.clone.clone.1 | custom fusion | bytes 2361344 | tf_op jit(solution)/shard_map/while/body/eval_jaxpr/jit(_take)/gather | solution.py:69
  23.7 3.4 %fusion.68 = f32[576,512]{0,1:T(8,128)S(1)} fusion(f32[576,512]{0,1:T(8,128)S(1)} %get-tuple-element.558, f32[512,576]{1,0:T(8,128)} %gather_fusion.3, f32[512,576]{1,0:T(8,128)} %gather_fusion.4, f32[512,576]{1,0:T(8,128)} %gather_fusion.5, f32[512,576]{1,0:T(8,128)} %gather_fusion.6, f32[512]{0:T(512)S(1)} %get-tuple-element.574, ...), kind=kLoop, calls=%fused_computation.40.clone.1 | loop fusion | flops 8552448 | bytes 7091520 | tf_op jit(solution)/shard_map/while/body/eval_jaxpr/jit(_where)/select_n | solution.py:77
  27.8 8.0 %collective-permute-start = (f32[576,128]{0,1:T(8,128)S(1)}, f32[576,128]{0,1:T(8,128)}, u32[]{:S(2)}, u32[]{:S(2)}) collective-permute-start(f32[576,128]{0,1:T(8,128)S(1)} %get-tuple-element.533), channel_id=1, source_target_pairs={{0,1},{1,2},{2,3},{4,5},{5,6},{6,7},{8,9},{9,10},{10,11},{12,13},{... | collective-permute-start | bytes 884744 | tf_op jit(solution)/shard_map/while/body/eval_jaxpr/ppermute | solution.py:27
  38.3 1.3 collective-permute-done.1
  40.7 2.6 %gather_fusion.4 = f32[512,576]{1,0:T(8,128)} fusion(f32[576,768]{0,1:T(8,128)S(1)} %constant_dynamic-update-slice_fusion.8, s32[1024]{0:T(1024)S(1)} %get-tuple-element.538), kind=kCustom, calls=%fused_computation.5.clone.clone.1 | custom fusion | bytes 2361344 | tf_op jit(solution)/shard_map/while/body/eval_jaxpr/jit(_take)/gather | solution.py:68
  43.2 2.5 %gather_fusion.5 = f32[512,576]{1,0:T(8,128)} fusion(f32[576,768]{0,1:T(8,128)S(1)} %constant_dynamic-update-slice_fusion.8, s32[1024]{0:T(1024)S(1)} %get-tuple-element.541), kind=kCustom, calls=%fused_computation.4.clone.clone.1 | custom fusion | bytes 2361344 | tf_op jit(solution)/shard_map/while/body/eval_jaxpr/jit(_take)/gather | solution.py:67
  45.8 2.6 %gather_fusion.6 = f32[512,576]{1,0:T(8,128)} fusion(f32[576,768]{0,1:T(8,128)S(1)} %constant_dynamic-update-slice_fusion.8, s32[1024]{0:T(1024)S(1)} %get-tuple-element.542), kind=kCustom, calls=%fused_computation.clone.clone.1 | custom fusion | bytes 2361344 | tf_op jit(solution)/shard_map/while/body/eval_jaxpr/jit(_take)/gather | solution.py:66
  48.3 2.6 %gather_fusion.3 = f32[512,576]{1,0:T(8,128)} fusion(f32[576,768]{0,1:T(8,128)S(1)} %constant_dynamic-update-slice_fusion.8, s32[1024]{0:T(1024)S(1)} %get-tuple-element.537), kind=kCustom, calls=%fused_computation.6.clone.clone.1 | custom fusion | bytes 2361344 | tf_op jit(solution)/shard_map/while/body/eval_jaxpr/jit(_take)/gather | solution.py:69
  50.9 3.4 %fusion.68 = f32[576,512]{0,1:T(8,128)S(1)} fusion(f32[576,512]{0,1:T(8,128)S(1)} %get-tuple-element.558, f32[512,576]{1,0:T(8,128)} %gather_fusion.3, f32[512,576]{1,0:T(8,128)} %gather_fusion.4, f32[512,576]{1,0:T(8,128)} %gather_fusion.5, f32[512,576]{1,0:T(8,128)} %gather_fusion.6, f32[512]{0:T(512)S(1)} %get-tuple-element.574, ...), kind=kLoop, calls=%fused_computation.40.clone.1 | loop fusion | flops 8552448 | bytes 7091520 | tf_op jit(solution)/shard_map/while/body/eval_jaxpr/jit(_where)/select_n | solution.py:77
  55.0 6.8 %collective-permute-start = (f32[576,128]{0,1:T(8,128)S(1)}, f32[576,128]{0,1:T(8,128)}, u32[]{:S(2)}, u32[]{:S(2)}) collective-permute-start(f32[576,128]{0,1:T(8,128)S(1)} %get-tuple-element.533), channel_id=1, source_target_pairs={{0,1},{1,2},{2,3},{4,5},{5,6},{6,7},{8,9},{9,10},{10,11},{12,13},{... | collective-permute-start | bytes 884744 | tf_op jit(solution)/shard_map/while/body/eval_jaxpr/ppermute | solution.py:27
  64.3 1.3 collective-permute-done.1
  66.7 2.6 %gather_fusion.4 = f32[512,576]{1,0:T(8,128)} fusion(f32[576,768]{0,1:T(8,128)S(1)} %constant_dynamic-update-slice_fusion.8, s32[1024]{0:T(1024)S(1)} %get-tuple-element.538), kind=kCustom, calls=%fused_computation.5.clone.clone.1 | custom fusion | bytes 2361344 | tf_op jit(solution)/shard_map/while/body/eval_jaxpr/jit(_take)/gather | solution.py:68
  69.2 2.5 %gather_fusion.5 = f32[512,576]{1,0:T(8,128)} fusion(f32[576,768]{0,1:T(8,128)S(1)} %constant_dynamic-update-slice_fusion.8, s32[1024]{0:T(1024)S(1)} %get-tuple-element.541), kind=kCustom, calls=%fused_computation.4.clone.clone.1 | custom fusion | bytes 2361344 | tf_op jit(solution)/shard_map/while/body/eval_jaxpr/jit(_take)/gather | solution.py:67
  71.8 2.6 %gather_fusion.6 = f32[512,576]{1,0:T(8,128)} fusion(f32[576,768]{0,1:T(8,128)S(1)} %constant_dynamic-update-slice_fusion.8, s32[1024]{0:T(1024)S(1)} %get-tuple-element.542), kind=kCustom, calls=%fused_computation.clone.clone.1 | custom fusion | bytes 2361344 | tf_op jit(solution)/shard_map/while/body/eval_jaxpr/jit(_take)/gather | solution.py:66
  74.4 2.6 %gather_fusion.3 = f32[512,576]{1,0:T(8,128)} fusion(f32[576,768]{0,1:T(8,128)S(1)} %constant_dynamic-update-slice_fusion.8, s32[1024]{0:T(1024)S(1)} %get-tuple-element.537), kind=kCustom, calls=%fused_computation.6.clone.clone.1 | custom fusion | bytes 2361344 | tf_op jit(solution)/shard_map/while/body/eval_jaxpr/jit(_take)/gather | solution.py:69
  76.9 3.4 %fusion.68 = f32[576,512]{0,1:T(8,128)S(1)} fusion(f32[576,512]{0,1:T(8,128)S(1)} %get-tuple-element.558, f32[512,576]{1,0:T(8,128)} %gather_fusion.3, f32[512,576]{1,0:T(8,128)} %gather_fusion.4, f32[512,576]{1,0:T(8,128)} %gather_fusion.5, f32[512,576]{1,0:T(8,128)} %gather_fusion.6, f32[512]{0:T(512)S(1)} %get-tuple-element.574, ...), kind=kLoop, calls=%fused_computation.40.clone.1 | loop fusion | flops 8552448 | bytes 7091520 | tf_op jit(solution)/shard_map/while/body/eval_jaxpr/jit(_where)/select_n | solution.py:77
  81.1 6.8 %collective-permute-start = (f32[576,128]{0,1:T(8,128)S(1)}, f32[576,128]{0,1:T(8,128)}, u32[]{:S(2)}, u32[]{:S(2)}) collective-permute-start(f32[576,128]{0,1:T(8,128)S(1)} %get-tuple-element.533), channel_id=1, source_target_pairs={{0,1},{1,2},{2,3},{4,5},{5,6},{6,7},{8,9},{9,10},{10,11},{12,13},{... | collective-permute-start | bytes 884744 | tf_op jit(solution)/shard_map/while/body/eval_jaxpr/ppermute | solution.py:27
  90.4 1.3 collective-permute-done.1
  92.7 2.6 %gather_fusion.4 = f32[512,576]{1,0:T(8,128)} fusion(f32[576,768]{0,1:T(8,128)S(1)} %constant_dynamic-update-slice_fusion.8, s32[1024]{0:T(1024)S(1)} %get-tuple-element.538), kind=kCustom, calls=%fused_computation.5.clone.clone.1 | custom fusion | bytes 2361344 | tf_op jit(solution)/shard_map/while/body/eval_jaxpr/jit(_take)/gather | solution.py:68
  95.3 2.5 %gather_fusion.5 = f32[512,576]{1,0:T(8,128)} fusion(f32[576,768]{0,1:T(8,128)S(1)} %constant_dynamic-update-slice_fusion.8, s32[1024]{0:T(1024)S(1)} %get-tuple-element.541), kind=kCustom, calls=%fused_computation.4.clone.clone.1 | custom fusion | bytes 2361344 | tf_op jit(solution)/shard_map/while/body/eval_jaxpr/jit(_take)/gather | solution.py:67
  97.8 2.6 %gather_fusion.6 = f32[512,576]{1,0:T(8,128)} fusion(f32[576,768]{0,1:T(8,128)S(1)} %constant_dynamic-update-slice_fusion.8, s32[1024]{0:T(1024)S(1)} %get-tuple-element.542), kind=kCustom, calls=%fused_computation.clone.clone.1 | custom fusion | bytes 2361344 | tf_op jit(solution)/shard_map/while/body/eval_jaxpr/jit(_take)/gather | solution.py:66
  100.4 2.6 %gather_fusion.3 = f32[512,576]{1,0:T(8,128)} fusion(f32[576,768]{0,1:T(8,128)S(1)} %constant_dynamic-update-slice_fusion.8, s32[1024]{0:T(1024)S(1)} %get-tuple-element.537), kind=kCustom, calls=%fused_computation.6.clone.clone.1 | custom fusion | bytes 2361344 | tf_op jit(solution)/shard_map/while/body/eval_jaxpr/jit(_take)/gather | solution.py:69
  102.9 3.4 %fusion.68 = f32[576,512]{0,1:T(8,128)S(1)} fusion(f32[576,512]{0,1:T(8,128)S(1)} %get-tuple-element.558, f32[512,576]{1,0:T(8,128)} %gather_fusion.3, f32[512,576]{1,0:T(8,128)} %gather_fusion.4, f32[512,576]{1,0:T(8,128)} %gather_fusion.5, f32[512,576]{1,0:T(8,128)} %gather_fusion.6, f32[512]{0:T(512)S(1)} %get-tuple-element.574, ...), kind=kLoop, calls=%fused_computation.40.clone.1 | loop fusion | flops 8552448 | bytes 7091520 | tf_op jit(solution)/shard_map/while/body/eval_jaxpr/jit(_where)/select_n | solution.py:77
  106.3 1.4 copy.33
  107.7 5.0 %all-to-all-start = ((f32[576,4,128]{2,0,1:T(8,128)}), f32[576,4,128]{2,0,1:T(8,128)}, u32[]{:S(2)}, u32[]{:S(2)}) async-start(f32[576,4,128]{2,0,1:T(8,128)} %copy.33), calls=%async_computation | async-start | bytes 2359296 | tf_op jit(solution)/shard_map/all_to_all | solution.py:85
  112.9 28.9 %all-to-all-done = f32[576,4,128]{2,0,1:T(8,128)} async-done(((f32[576,4,128]{2,0,1:T(8,128)}), f32[576,4,128]{2,0,1:T(8,128)}, u32[]{:S(2)}, u32[]{:S(2)}) %all-to-all-start) | async-done | bytes 1179680 | tf_op jit(solution)/shard_map/all_to_all | solution.py:85
  141.8 1.4 convert_element_type.21
  144.3 24.0 %while.25 = (s32[]{:T(128)}, f32[36,64,128]{2,1,0:T(8,128)}, s32[2,4,32]{2,0,1:T(2,128)S(1)}, f32[2,32]{1,0:T(2,128)S(1)}, bf16[2,32,64,64]{3,2,1,0:T(8,128)(2,1...) while((s32[]{:T(128)}, f32[36,64,128]{2,1,0:T(8,128)}, ...), condition=%wide.region_5.7_spmd, body=%wide.region_3.6_spmd.sunk | while | flops 101977472 | bytes 18891668 | solution.py:125
  144.3 1.4 gather_fusion.2
  145.8 1.9 gather_fusion
  148.3 1.3 fusion.64
  149.7 1.8 convolution_multiply_fusion.3
  151.5 4.8 %scatter_fusion = f32[36,64,128]{2,1,0:T(8,128)} fusion(f32[36,64,128]{2,1,0:T(8,128)} %get-tuple-element.586, s32[32]{0:T(128)S(1)} %get-tuple-element.518, f32[32,64,128]{2,1,0:T(8,128)S(1)} %convolution_multiply_fusion.3), kind=kCustom, calls=%fused_computation.7.clone.1 | custom fusion | flops 262144 | bytes 3145856 | tf_op jit(solution)/shard_map/while/body/eval_jaxpr/scatter-add | solution.py:122
  156.4 1.4 gather_fusion.2
  157.8 1.9 gather_fusion
  160.3 1.3 fusion.64
  161.7 1.8 convolution_multiply_fusion.3
  163.5 4.8 %scatter_fusion = f32[36,64,128]{2,1,0:T(8,128)} fusion(f32[36,64,128]{2,1,0:T(8,128)} %get-tuple-element.586, s32[32]{0:T(128)S(1)} %get-tuple-element.518, f32[32,64,128]{2,1,0:T(8,128)S(1)} %convolution_multiply_fusion.3), kind=kCustom, calls=%fused_computation.7.clone.1 | custom fusion | flops 262144 | bytes 3145856 | tf_op jit(solution)/shard_map/while/body/eval_jaxpr/scatter-add | solution.py:122
  168.3 1.8 multiply_add_fusion
  170.2 32.3 %all_to_all.30 = f32[2304,1,128]{2,1,0:T(1,128)S(1)} all-to-all(f32[2304,1,128]{2,1,0:T(1,128)S(1)} %bitcast.116), channel_id=1, replica_groups=mesh['grp'=2,'comp'=4,'space'=4] {'comp'}, dimensions={0} | all-to-all | bytes 2359296 | tf_op jit(solution)/shard_map/all_to_all | solution.py:92
  (102 shorter events, 21.7 us)
Async XLA Ops:
  0.0 3.3 %copy-start.3 = (f32[512]{0:T(512)S(1)}, f32[512]{0:T(512)}, u32[]{:S(2)}) copy-start(f32[512]{0:T(512)} %param.17) | copy-start | bytes 6148
  0.0 3.3 %copy-start.4 = (f32[512]{0:T(512)S(1)}, f32[512]{0:T(512)}, u32[]{:S(2)}) copy-start(f32[512]{0:T(512)} %param.18) | copy-start | bytes 6148
  0.0 3.3 %copy-start.2 = (s32[4,512]{1,0:T(4,128)S(1)}, s32[4,512]{1,0:T(4,128)}, u32[]{:S(2)}) copy-start(s32[4,512]{1,0:T(4,128)} %param.20) | copy-start | bytes 24580
  4.1 4.5 %collective-permute-start = (f32[576,128]{0,1:T(8,128)S(1)}, f32[576,128]{0,1:T(8,128)}, u32[]{:S(2)}, u32[]{:S(2)}) collective-permute-start(f32[576,128]{0,1:T(8,128)S(1)} %get-tuple-element.533), channel_id=1, source_target_pairs={{0,1},{1,2},{2,3},{4,5},{5,6},{6,7},{8,9},{9,10},{10,11},{12,13},{... | collective-permute-start | bytes 884744 | tf_op jit(solution)/shard_map/while/body/eval_jaxpr/ppermute | solution.py:27
  7.2 5.2 %collective-permute-start.1 = (f32[576,128]{0,1:T(8,128)}, f32[576,128]{0,1:T(8,128)}, u32[]{:S(2)}, u32[]{:S(2)}) collective-permute-start(f32[576,128]{0,1:T(8,128)} %get-tuple-element.534), channel_id=1, source_target_pairs={{1,0},{2,1},{3,2},{5,4},{6,5},{7,6},{9,8},{10,9},{11,10},{13,12},{... | collective-permute-start | bytes 884744 | tf_op jit(solution)/shard_map/while/body/eval_jaxpr/ppermute | solution.py:29
  27.8 9.4 %collective-permute-start = (f32[576,128]{0,1:T(8,128)S(1)}, f32[576,128]{0,1:T(8,128)}, u32[]{:S(2)}, u32[]{:S(2)}) collective-permute-start(f32[576,128]{0,1:T(8,128)S(1)} %get-tuple-element.533), channel_id=1, source_target_pairs={{0,1},{1,2},{2,3},{4,5},{5,6},{6,7},{8,9},{9,10},{10,11},{12,13},{... | collective-permute-start | bytes 884744 | tf_op jit(solution)/shard_map/while/body/eval_jaxpr/ppermute | solution.py:27
  35.8 3.9 %collective-permute-start.1 = (f32[576,128]{0,1:T(8,128)}, f32[576,128]{0,1:T(8,128)}, u32[]{:S(2)}, u32[]{:S(2)}) collective-permute-start(f32[576,128]{0,1:T(8,128)} %get-tuple-element.534), channel_id=1, source_target_pairs={{1,0},{2,1},{3,2},{5,4},{6,5},{7,6},{9,8},{10,9},{11,10},{13,12},{... | collective-permute-start | bytes 884744 | tf_op jit(solution)/shard_map/while/body/eval_jaxpr/ppermute | solution.py:29
  55.0 8.2 %collective-permute-start = (f32[576,128]{0,1:T(8,128)S(1)}, f32[576,128]{0,1:T(8,128)}, u32[]{:S(2)}, u32[]{:S(2)}) collective-permute-start(f32[576,128]{0,1:T(8,128)S(1)} %get-tuple-element.533), channel_id=1, source_target_pairs={{0,1},{1,2},{2,3},{4,5},{5,6},{6,7},{8,9},{9,10},{10,11},{12,13},{... | collective-permute-start | bytes 884744 | tf_op jit(solution)/shard_map/while/body/eval_jaxpr/ppermute | solution.py:27
  61.8 3.9 %collective-permute-start.1 = (f32[576,128]{0,1:T(8,128)}, f32[576,128]{0,1:T(8,128)}, u32[]{:S(2)}, u32[]{:S(2)}) collective-permute-start(f32[576,128]{0,1:T(8,128)} %get-tuple-element.534), channel_id=1, source_target_pairs={{1,0},{2,1},{3,2},{5,4},{6,5},{7,6},{9,8},{10,9},{11,10},{13,12},{... | collective-permute-start | bytes 884744 | tf_op jit(solution)/shard_map/while/body/eval_jaxpr/ppermute | solution.py:29
  81.1 8.2 %collective-permute-start = (f32[576,128]{0,1:T(8,128)S(1)}, f32[576,128]{0,1:T(8,128)}, u32[]{:S(2)}, u32[]{:S(2)}) collective-permute-start(f32[576,128]{0,1:T(8,128)S(1)} %get-tuple-element.533), channel_id=1, source_target_pairs={{0,1},{1,2},{2,3},{4,5},{5,6},{6,7},{8,9},{9,10},{10,11},{12,13},{... | collective-permute-start | bytes 884744 | tf_op jit(solution)/shard_map/while/body/eval_jaxpr/ppermute | solution.py:27
  87.8 3.9 %collective-permute-start.1 = (f32[576,128]{0,1:T(8,128)}, f32[576,128]{0,1:T(8,128)}, u32[]{:S(2)}, u32[]{:S(2)}) collective-permute-start(f32[576,128]{0,1:T(8,128)} %get-tuple-element.534), channel_id=1, source_target_pairs={{1,0},{2,1},{3,2},{5,4},{6,5},{7,6},{9,8},{10,9},{11,10},{13,12},{... | collective-permute-start | bytes 884744 | tf_op jit(solution)/shard_map/while/body/eval_jaxpr/ppermute | solution.py:29
  107.7 5.0 %copy-start.5 = (s32[4,64]{1,0:T(4,128)S(1)}, s32[4,64]{1,0:T(4,128)}, u32[]{:S(2)}) copy-start(s32[4,64]{1,0:T(4,128)} %param.22) | copy-start | bytes 3076
  107.7 5.1 %copy-start.6 = (f32[64]{0:T(128)S(1)}, f32[64]{0:T(128)}, u32[]{:S(2)}) copy-start(f32[64]{0:T(128)} %param.23) | copy-start | bytes 772
  107.7 34.1 %all-to-all-start = ((f32[576,4,128]{2,0,1:T(8,128)}), f32[576,4,128]{2,0,1:T(8,128)}, u32[]{:S(2)}, u32[]{:S(2)}) async-start(f32[576,4,128]{2,0,1:T(8,128)} %copy.33), calls=%async_computation | async-start | bytes 2359296 | tf_op jit(solution)/shard_map/all_to_all | solution.py:85
  144.3 3.4 %copy-start = (bf16[36,64,128]{2,1,0:T(8,128)(2,1)}, bf16[36,64,128]{2,1,0:T(8,128)(2,1)S(1)}, u32[]{:S(2)}) copy-start(bf16[36,64,128]{2,1,0:T(8,128)(2,1)S(1)} %get-tuple-element.598) | copy-start | bytes 1769476 | tf_op jit(solution)/shard_map/while
  151.5 4.8 %copy-start.1 = (bf16[36,64,128]{2,1,0:T(8,128)(2,1)S(1)}, bf16[36,64,128]{2,1,0:T(8,128)(2,1)}, u32[]{:S(2)}) copy-start(bf16[36,64,128]{2,1,0:T(8,128)(2,1)} %copy-done) | copy-start | bytes 1769476 | tf_op jit(solution)/shard_map/while
  156.3 3.4 %copy-start = (bf16[36,64,128]{2,1,0:T(8,128)(2,1)}, bf16[36,64,128]{2,1,0:T(8,128)(2,1)S(1)}, u32[]{:S(2)}) copy-start(bf16[36,64,128]{2,1,0:T(8,128)(2,1)S(1)} %get-tuple-element.598) | copy-start | bytes 1769476 | tf_op jit(solution)/shard_map/while
  163.5 4.8 %copy-start.1 = (bf16[36,64,128]{2,1,0:T(8,128)(2,1)S(1)}, bf16[36,64,128]{2,1,0:T(8,128)(2,1)}, u32[]{:S(2)}) copy-start(bf16[36,64,128]{2,1,0:T(8,128)(2,1)} %copy-done) | copy-start | bytes 1769476 | tf_op jit(solution)/shard_map/while
where the time goes:
time: 206 us; the launch traced here: 204 us
  local copies, waits for them, and re-layouts  66.6 us (32%)
  waiting for transfers between devices  35.6 us (17%)
  starting transfers between devices  34.7 us (17%)
  blocking collectives  32.3 us (16%)
  other arithmetic  28 us (14%)
  matrix products  6.35 us (3%)
    all_to_all x1, blocking collectives, to_components(): lax.all_to_all(pieces, 'comp', split_axis=0, concat_axis=1, tiled=True)  32.3 us
    all_to_all x1, waiting for transfers between devices, to_points(): lax.all_to_all(pieces, 'comp', split_axis=1, concat_axis=0, tiled=True)  28.9 us
    ppermute x4, starting transfers between devices, padded(): lax.ppermute(tail, axis, [(i, (i + 1) % count) for i in range(ends)])  24.6 us
    select_n x4, other arithmetic, sweep_once(): return jnp.where(repeat < counts[:, None], updated, values)  13.4 us
    gather x4, local copies, waits for them, and re-layouts, sweep_once(): south_value = jnp.take(extended, neighbours[2], axis=1)  10.3 us
    gather x4, local copies, waits for them, and re-layouts, sweep_once(): north_value = jnp.take(extended, neighbours[3], axis=1)  10.2 us
    gather x4, local copies, waits for them, and re-layouts, sweep_once(): west_value = jnp.take(extended, neighbours[0], axis=1)  10.2 us
    gather x4, local copies, waits for them, and re-layouts, sweep_once(): east_value = jnp.take(extended, neighbours[1], axis=1)  10.2 us
  transfers between devices with their start and end apart: 9, of which 5 were waited for; matrix products, arithmetic and copies ran while one was open for 2% of the time, Pallas kernels for 0%

commit v1 on v0

v1 whole, which is shorter than its diff:
```python
import functools
import math

import jax
import jax.numpy as jnp
import numpy as np
from jax import lax
from jax.experimental import pallas as pl
from jax.experimental.pallas import tpu as pltpu
from jax.sharding import PartitionSpec as P

NF = 36
ND = 64
SUB = 4
HALO = 128
SKEW = 2

courant_scale = 0.4
courant_limit = 0.45
source_step = 0.1

MESH = pl.DeviceIdType.MESH


def chunk_rows(rows):
    for size in (64, 72, 48, 40, 32, 24, 16, 8):
        if rows % size == 0:
            return size
    return rows


def sync(peers, spaces):
    me = lax.axis_index("comp")
    here = lax.axis_index("space")
    barrier = pltpu.get_barrier_semaphore()
    count = 0
    for k in range(1, peers):
        pl.semaphore_signal(
            barrier, inc=1, device_id={"comp": lax.rem(me + k, peers)}, device_id_type=MESH
        )
        count += 1
    if spaces:
        for k in (1, spaces - 1):
            pl.semaphore_signal(
                barrier, inc=1, device_id={"space": lax.rem(here + k, spaces)}, device_id_type=MESH
            )
            count += 1
    pl.semaphore_wait(barrier, count)


def propagate_kernel(
    peers,
    spaces,
    chunk,
    field_ref,
    columns_ref,
    current_ref,
    position_ref,
    points_ref,
    states,
    speed_x,
    speed_y,
    load_sem,
    halo_send,
    halo_recv,
    piece_send,
    piece_recv,
    own_sem,
):
    me = lax.axis_index("comp")
    here = lax.axis_index("space")
    rows = columns_ref.shape[0]
    tiles = position_ref.shape[0]
    chunks = rows // chunk
    has_left = here > 0
    has_right = here < spaces - 1

    loads = [
        pltpu.make_async_copy(
            field_ref.at[:, pl.ds(j * HALO, HALO)], states.at[0, j + 1], load_sem.at[j]
        )
        for j in range(tiles)
    ]
    for load in loads:
        load.start()

    @pl.when(jnp.logical_not(has_left))
    def _():
        for s in range(SUB):
            states[s, 0] = jnp.zeros((rows, HALO), jnp.float32)

    @pl.when(jnp.logical_not(has_right))
    def _():
        for s in range(SUB):
            states[s, tiles + 1] = jnp.zeros((rows, HALO), jnp.float32)

    sync(peers, spaces)

    def halo_copies(s, first, count):
        part = pl.ds(first, count)
        chunk_id = first // chunk
        to_left = pltpu.make_async_remote_copy(
            src_ref=states.at[s, 1, part],
            dst_ref=states.at[s, tiles + 1, part],
            send_sem=halo_send.at[s, 0],
            recv_sem=halo_recv.at[s, 0, chunk_id],
            device_id={"space": jnp.maximum(here - 1, 0)},
            device_id_type=MESH,
        )
        to_right = pltpu.make_async_remote_copy(
            src_ref=states.at[s, tiles, part],
            dst_ref=states.at[s, 0, part],
            send_sem=halo_send.at[s, 1],
            recv_sem=halo_recv.at[s, 1, chunk_id],
            device_id={"space": jnp.minimum(here + 1, spaces - 1)},
            device_id_type=MESH,
        )
        return to_left, to_right

    def send_halo(s, c):
        to_left, to_right = halo_copies(s, c * chunk, chunk)

        @pl.when(has_left)
        def _():
            to_left.start()

        @pl.when(has_right)
        def _():
            to_right.start()

    def wait_halo(s, c):
        to_left, to_right = halo_copies(s, c * chunk, chunk)

        @pl.when(has_right)
        def _():
            to_left.wait_recv()

        @pl.when(has_left)
        def _():
            to_right.wait_recv()

    def piece(k, first, count):
        target = lax.rem(me + k, peers)
        return pltpu.make_async_remote_copy(
            src_ref=states.at[SUB, target + 1, pl.ds(first, count)],
            dst_ref=points_ref.at[pl.ds(pl.multiple_of(me * rows + first, 8), count)],
            send_sem=piece_send.at[k],
            recv_sem=piece_recv.at[k],
            device_id={"comp": target},
            device_id_type=MESH,
        )

    order = sorted(range(1, peers), key=lambda k: abs(k - peers / 2))

    def send_pieces(c):
        for k in order:
            piece(k, c * chunk, chunk).start()

    def prepare(c):
        def per_tile(j, carry):
            east = jnp.broadcast_to(current_ref[j, 0:1, :], (8, HALO))
            north = jnp.broadcast_to(current_ref[j, 1:2, :], (8, HALO))

            def per_group(g, inner):
                at = pl.ds(pl.multiple_of(c * chunk + g * 8, 8), 8)
                values = columns_ref[at, :]
                scale = values[:, 2:3]
                along_x = (values[:, 0:1] + east) * scale
                along_y = (values[:, 1:2] + north) * scale
                speed_x[j, at] = jnp.clip(along_x, -courant_limit, courant_limit)
                speed_y[j, at] = jnp.clip(along_y, -courant_limit, courant_limit)
                return inner

            return lax.fori_loop(0, chunk // 8, per_group, carry, unroll=True)

        lax.fori_loop(0, tiles, per_tile, 0)

    def advance(s, c):
        def per_tile(j, carry):
            west, east, south, north = [
                jnp.broadcast_to(position_ref[j, d : d + 1, :], (8, HALO)) for d in range(4)
            ]

            def upwind(speed, near, far, before, here_tile, after):
                spot = jnp.where(speed > 0.0, near, far)
                lane = spot & (HALO - 1)
                taken = [
                    jnp.take_along_axis(tile, lane, axis=1, mode="promise_in_bounds")
                    for tile in (before, here_tile, after)
                ]
                value = jnp.where(
                    spot < HALO, taken[0], jnp.where(spot < 2 * HALO, taken[1], taken[2])
                )
                return jnp.abs(speed) * (here_tile - value)

            def per_group(g, inner):
                at = pl.ds(pl.multiple_of(c * chunk + g * 8, 8), 8)
                before = states[s, j, at]
                value = states[s, j + 1, at]
                after = states[s, j + 2, at]
                change = upwind(speed_x[j, at], west, east, before, value, after)
                change = change + upwind(speed_y[j, at], south, north, before, value, after)
                live = columns_ref[at, :][:, 3:4] > float(s)
                states[s + 1, j + 1, at] = jnp.where(live, value - change, value)
                return inner

            return lax.fori_loop(0, chunk // 8, per_group, carry, unroll=True)

        lax.fori_loop(0, tiles, per_tile, 0)

    for load in loads:
        load.wait()
    for c in range(chunks):
        send_halo(0, c)
    for wave in range(chunks + SKEW * (SUB - 1)):
        for s in reversed(range(SUB)):
            c = wave - SKEW * s
            if not 0 <= c < chunks:
                continue
            if s == 0:
                prepare(c)
            wait_halo(s, c)
            advance(s, c)
            if s + 1 < SUB:
                send_halo(s + 1, c)
            else:
                send_pieces(c)
    own = pltpu.make_async_copy(
        states.at[SUB, me + 1],
        points_ref.at[pl.ds(pl.multiple_of(me * rows, 8), rows)],
        own_sem,
    )
    own.start()
    own.wait()
    for s in range(SUB):
        to_left, to_right = halo_copies(s, 0, rows)

        @pl.when(has_left)
        def _():
            to_left.wait_send()

        @pl.when(has_right)
        def _():
            to_right.wait_send()

    for k in range(1, peers):
        whole = piece(k, 0, rows)
        whole.wait_send()
        whole.wait_recv()


def propagate(field, columns, current, position, peers, spaces):
    rows = field.shape[0]
    tiles = position.shape[0]
    chunk = chunk_rows(rows)
    vmem = pl.BlockSpec(memory_space=pltpu.VMEM)
    return pl.pallas_call(
        functools.partial(propagate_kernel, peers, spaces, chunk),
        out_shape=jax.ShapeDtypeStruct((peers * rows, HALO), jnp.float32),
        in_specs=[pl.BlockSpec(memory_space=pl.ANY), vmem, vmem, vmem],
        out_specs=vmem,
        scratch_shapes=[
            pltpu.VMEM((SUB + 1, tiles + 2, rows, HALO), jnp.float32),
            pltpu.VMEM((tiles, rows, HALO), jnp.float32),
            pltpu.VMEM((tiles, rows, HALO), jnp.float32),
            pltpu.SemaphoreType.DMA((tiles,)),
            pltpu.SemaphoreType.DMA((SUB, 2)),
            pltpu.SemaphoreType.DMA((SUB, 2, rows // chunk)),
            pltpu.SemaphoreType.DMA((peers,)),
            pltpu.SemaphoreType.DMA((peers,)),
            pltpu.SemaphoreType.DMA,
        ],
        compiler_params=pltpu.CompilerParams(collective_id=0, has_side_effects=True),
    )(field, columns, current, position)


def source_kernel(batch, quad_ref, strength_ref, points_ref, blocks_ref, out_ref, rounded):
    total = blocks_ref.shape[0]

    def fill(f, carry):
        value = points_ref[f]
        rounded[f] = value.astype(jnp.bfloat16)
        out_ref[f] = value
        return carry

    lax.fori_loop(0, NF, fill, 0, unroll=4)

    def step(i, carry):
        parts = []
        for b in range(batch):
            j = i * batch + b
            block = blocks_ref[j]
            left = jnp.dot(block, rounded[quad_ref[0, j]], preferred_element_type=jnp.float32)
            right = lax.dot_general(
                block,
                rounded[quad_ref[1, j]],
                (((0,), (0,)), ((), ())),
                preferred_element_type=jnp.float32,
            )
            product = (left * right * points_ref[quad_ref[2, j]]).astype(jnp.bfloat16)
            part = jnp.dot(block, product, preferred_element_type=jnp.float32)
            parts.append(part * (strength_ref[j] * source_step))
        for b in range(batch):
            target = quad_ref[3, i * batch + b]
            out_ref[target] = out_ref[target] + parts[b]
        return carry

    lax.fori_loop(0, total // batch, step, 0)


def source_term(points, blocks, quad_index, strength):
    width = points.shape[1]
    vmem = pl.BlockSpec(memory_space=pltpu.VMEM)
    smem = pl.BlockSpec(memory_space=pltpu.SMEM)
    out = pl.pallas_call(
        functools.partial(source_kernel, math.gcd(blocks.shape[0], 4)),
        out_shape=jax.ShapeDtypeStruct((NF, ND, width), jnp.float32),
        in_specs=[smem, smem, vmem, vmem],
        out_specs=vmem,
        scratch_shapes=[pltpu.VMEM((NF, ND, width), jnp.bfloat16)],
    )(quad_index, strength, points.reshape(NF, ND, width), blocks)
    return out.reshape(NF * ND, width)


def home_kernel(peers, points_ref, out_ref, send_sem, recv_sem, own_sem):
    me = lax.axis_index("comp")
    rows = out_ref.shape[0]
    place = pl.ds(pl.multiple_of(me * HALO, HALO), HALO)
    own = pltpu.make_async_copy(
        points_ref.at[pl.ds(pl.multiple_of(me * rows, 8), rows)], out_ref.at[:, place], own_sem
    )
    own.start()
    sync(peers, 0)
    copies = []
    for k in sorted(range(1, peers), key=lambda k: abs(k - peers / 2)):
        target = lax.rem(me + k, peers)
        copy = pltpu.make_async_remote_copy(
            src_ref=points_ref.at[pl.ds(pl.multiple_of(target * rows, 8), rows)],
            dst_ref=out_ref.at[:, place],
            send_sem=send_sem.at[k],
            recv_sem=recv_sem.at[k],
            device_id={"comp": target},
            device_id_type=MESH,
        )
        copy.start()
        copies.append(copy)
    own.wait()
    for copy in copies:
        copy.wait()


def send_home(points, peers):
    rows = points.shape[0] // peers
    return pl.pallas_call(
        functools.partial(home_kernel, peers),
        out_shape=jax.ShapeDtypeStruct((rows, peers * HALO), jnp.float32),
        in_specs=[pl.BlockSpec(memory_space=pltpu.VMEM)],
        out_specs=pl.BlockSpec(memory_space=pltpu.VMEM),
        scratch_shapes=[
            pltpu.SemaphoreType.DMA((peers,)),
            pltpu.SemaphoreType.DMA((peers,)),
            pltpu.SemaphoreType.DMA,
        ],
        compiler_params=pltpu.CompilerParams(collective_id=1, has_side_effects=True),
    )(points)


def shards(
    spectrum,
    wave_speed,
    current_east,
    current_north,
    substeps,
    neighbours,
    blocks,
    quad_index,
    strength,
):
    peers = lax.axis_size("comp")
    spaces = lax.axis_size("space")
    rows, width = spectrum.shape
    assert width == peers * HALO
    first = lax.axis_index("comp") * rows
    angles = (np.arange(ND, dtype=np.float32) + np.float32(0.5)) * np.float32(2.0 * math.pi / ND)
    counts = substeps.astype(jnp.float32)
    columns = jnp.stack(
        [
            (wave_speed[:, None] * np.cos(angles)[None, :]).reshape(NF * ND),
            (wave_speed[:, None] * np.sin(angles)[None, :]).reshape(NF * ND),
            courant_scale / counts,
            counts,
        ],
        axis=1,
    )
    columns = lax.dynamic_slice_in_dim(columns, first, rows)
    tiles = width // HALO
    current = jnp.stack(
        [current_east.reshape(tiles, HALO), current_north.reshape(tiles, HALO)], axis=1
    )
    position = neighbours.reshape(4, tiles, HALO) - HALO * jnp.arange(tiles)[None, :, None]
    position = position.transpose(1, 0, 2)
    points = propagate(spectrum, columns, current, position, peers, spaces)
    points = source_term(points, blocks, quad_index, strength)
    return send_home(points, peers)


def solution(mesh):
    in_specs = (
        P("comp", ("grp", "space")),
        P(),
        P(("grp", "space")),
        P(("grp", "space")),
        P(),
        P(None, ("grp", "space")),
        P(),
        P(),
        P(),
    )
    out_specs = P("comp", ("grp", "space"))
    return jax.shard_map(shards, mesh=mesh, in_specs=in_specs, out_specs=out_specs, check_vma=False)
```

time: 206 us -> 103 us (0.50)
  the two profiles are of different devices: /device:TPU:0 before, /device:TPU:12 now
where the time goes in v1:
time: 103 us
  Pallas kernels  94.5 us (92%)
  other arithmetic  4.93 us (5%)
  local copies, waits for them, and re-layouts  3.43 us (3%)
    pallas_call x1, Pallas kernels, propagate(): pl.pallas_call(functools.partial(propagate_kernel, peers, spaces, chunk),...  49.1 us
    pallas_call x1, Pallas kernels, send_home(): pl.pallas_call(functools.partial(home_kernel, peers), out_shape=jax.Shape...  31.2 us
    pallas_call x1, Pallas kernels, source_term(): pl.pallas_call(functools.partial(source_kernel, math.gcd(blocks.shape[0],...  14.1 us
    unnamed x2, local copies, waits for them, and re-layouts  3.25 us

profile of v1, /device:TPU:12, one launch (start us, length us, event | category | flops | bytes accessed | tf_op | source)
XLA Modules:
  0.0 102.9 jit_solution(8195514261083467281)
XLA Ops:
  0.0 1.3 %pad_maximum_fusion.current_ref = f32[4,2,128]{2,1,0:T(2,128)} fusion(f32[4,1,128]{2,1,0:T(1,128)} %bitcast.12, f32[4,1,128]{2,1,0:T(1,128)} %bitcast.13), kind=kLoop, calls=%fused_computation.12 | loop fusion | flops 1024 | bytes 8192 | tf_op jit(solution)/shard_map/stack | solution.py:397
  1.3 1.4 %fusion.3.position_ref = s32[4,4,128]{2,1,0:T(4,128)} fusion(s32[4,512]{1,0:T(4,128)} %param.16, s32[4]{0:T(128)S(1)} %iota_multiply_fusion), kind=kLoop, calls=%fused_computation.10 | loop fusion | flops 2048 | bytes 16400 | tf_op jit(solution)/shard_map/transpose | solution.py:401
  2.7 0.7 broadcast_divide_fusion
  3.4 0.7 convert_element_type.3
  4.1 0.8 broadcast_multiply_fusion
  4.9 0.1 mul.67
  5.0 0.1 mul.63
  5.0 0.1 fusion.2
  5.1 0.9 copy.17.columns_ref
  6.0 49.1 %shard_map.109 = f32[2304,128]{1,0:T(8,128)} custom-call(f32[576,512]{1,0:T(8,128)} %field_ref.1, f32[576,4]{1,0:T(8,128)} %copy.17.columns_ref, f32[4,2,128]{2,1,0:T(2,128)} %pad_maximum_fusion.current_ref, s32[4,4,128]{2,1,0:T(4,128)} %fusion.3.position_ref), custom_call_target="tpu_custom_call" | custom-call | tf_op jit(solution)/shard_map/pallas_call | solution.py:257
  55.2 14.1 %shard_map.110 = f32[36,64,128]{2,1,0:T(8,128)} custom-call(s32[4,64]{1,0:T(4,128)} %quad_ref.1, f32[64]{0:T(128)} %strength_ref.1, f32[36,64,128]{2,1,0:T(8,128)} %bitcast.10, bf16[64,64,64]{2,1,0:T(8,128)(2,1)} %blocks_ref.1), custom_call_target="tpu_custom_call" | custom-call | tf_op jit(solution)/shard_map/pallas_call | solution.py:315
  69.2 31.2 %shard_map.111 = f32[576,512]{1,0:T(8,128)} custom-call(f32[2304,128]{1,0:T(8,128)} %bitcast.11), custom_call_target="tpu_custom_call" | custom-call | tf_op jit(solution)/shard_map/pallas_call | solution.py:354
  100.5 2.4 %copy.19 = f32[576,512]{1,0:T(8,128)} copy(f32[576,512]{1,0:T(8,128)} %shard_map.111) | data formatting | bytes 2359296
  (3 shorter events, 0.0 us)

commit v2 on v1

--- a/solution.py
+++ b/solution.py
@@ -13,7 +13,7 @@
 ND = 64
 SUB = 4
 HALO = 128
-SKEW = 2
+SKEW = 1
 
 courant_scale = 0.4
 courant_limit = 0.45
@@ -53,13 +53,17 @@
     spaces,
     chunk,
     field_ref,
-    columns_ref,
-    current_ref,
-    position_ref,
+    wave_ref,
+    substeps_ref,
+    trig_ref,
+    east_ref,
+    north_ref,
+    neighbour_ref,
     points_ref,
     states,
     speed_x,
     speed_y,
+    repeats,
     load_sem,
     halo_send,
     halo_recv,
@@ -69,8 +73,8 @@
 ):
     me = lax.axis_index("comp")
     here = lax.axis_index("space")
-    rows = columns_ref.shape[0]
-    tiles = position_ref.shape[0]
+    rows, width = field_ref.shape
+    tiles = width // HALO
     chunks = rows // chunk
     has_left = here > 0
     has_right = here < spaces - 1
@@ -156,29 +160,43 @@
         for k in order:
             piece(k, c * chunk, chunk).start()
 
+    def lanes(j):
+        return pl.ds(pl.multiple_of(j * HALO, HALO), HALO)
+
+    sublane = lax.broadcasted_iota(jnp.int32, (8, HALO), 0)
+
     def prepare(c):
-        def per_tile(j, carry):
-            east = jnp.broadcast_to(current_ref[j, 0:1, :], (8, HALO))
-            north = jnp.broadcast_to(current_ref[j, 1:2, :], (8, HALO))
-
-            def per_group(g, inner):
-                at = pl.ds(pl.multiple_of(c * chunk + g * 8, 8), 8)
-                values = columns_ref[at, :]
-                scale = values[:, 2:3]
-                along_x = (values[:, 0:1] + east) * scale
-                along_y = (values[:, 1:2] + north) * scale
+        def per_group(g, carry):
+            row = pl.multiple_of(c * chunk + g * 8, 8)
+            at = pl.ds(row, 8)
+            component = me * rows + row
+            speed = wave_ref[component // ND]
+            turn = pl.ds(pl.multiple_of(lax.rem(component, ND), 8), 8)
+            own_x = trig_ref[0, turn, :] * speed
+            own_y = trig_ref[1, turn, :] * speed
+            taken = jnp.full((8, HALO), substeps_ref[component], jnp.int32)
+            for i in range(1, 8):
+                taken = jnp.where(sublane == i, substeps_ref[component + i], taken)
+            count = taken.astype(jnp.float32)
+            repeats[at] = count
+            scale = courant_scale / count
+
+            def per_tile(j, inner):
+                along_x = (own_x + east_ref[0:1, lanes(j)]) * scale
+                along_y = (own_y + north_ref[0:1, lanes(j)]) * scale
                 speed_x[j, at] = jnp.clip(along_x, -courant_limit, courant_limit)
                 speed_y[j, at] = jnp.clip(along_y, -courant_limit, courant_limit)
                 return inner
 
-            return lax.fori_loop(0, chunk // 8, per_group, carry, unroll=True)
-
-        lax.fori_loop(0, tiles, per_tile, 0)
+            return lax.fori_loop(0, tiles, per_tile, carry, unroll=tiles <= 4)
+
+        lax.fori_loop(0, chunk // 8, per_group, 0)
 
     def advance(s, c):
         def per_tile(j, carry):
             west, east, south, north = [
-                jnp.broadcast_to(position_ref[j, d : d + 1, :], (8, HALO)) for d in range(4)
+                jnp.broadcast_to(neighbour_ref[d : d + 1, lanes(j)] - j * HALO, (8, HALO))
+                for d in range(4)
             ]
 
             def upwind(speed, near, far, before, here_tile, after):
@@ -200,8 +218,9 @@
                 after = states[s, j + 2, at]
                 change = upwind(speed_x[j, at], west, east, before, value, after)
                 change = change + upwind(speed_y[j, at], south, north, before, value, after)
-                live = columns_ref[at, :][:, 3:4] > float(s)
-                states[s + 1, j + 1, at] = jnp.where(live, value - change, value)
+                if s > 0:
+                    change = jnp.where(repeats[at] > float(s), change, 0.0)
+                states[s + 1, j + 1, at] = value - change
                 return inner
 
             return lax.fori_loop(0, chunk // 8, per_group, carry, unroll=True)
@@ -249,20 +268,25 @@
         whole.wait_recv()
 
 
-def propagate(field, columns, current, position, peers, spaces):
-    rows = field.shape[0]
-    tiles = position.shape[0]
+def propagate(field, wave_speed, substeps, east, north, neighbours, peers, spaces):
+    rows, width = field.shape
+    tiles = width // HALO
     chunk = chunk_rows(rows)
+    angles = (np.arange(ND, dtype=np.float32) + np.float32(0.5)) * np.float32(2.0 * math.pi / ND)
+    trig = np.stack([np.cos(angles), np.sin(angles)])
+    trig = np.ascontiguousarray(np.broadcast_to(trig[:, :, None], (2, ND, HALO)))
     vmem = pl.BlockSpec(memory_space=pltpu.VMEM)
+    smem = pl.BlockSpec(memory_space=pltpu.SMEM)
     return pl.pallas_call(
         functools.partial(propagate_kernel, peers, spaces, chunk),
         out_shape=jax.ShapeDtypeStruct((peers * rows, HALO), jnp.float32),
-        in_specs=[pl.BlockSpec(memory_space=pl.ANY), vmem, vmem, vmem],
+        in_specs=[pl.BlockSpec(memory_space=pl.ANY), smem, smem, vmem, vmem, vmem, vmem],
         out_specs=vmem,
         scratch_shapes=[
             pltpu.VMEM((SUB + 1, tiles + 2, rows, HALO), jnp.float32),
             pltpu.VMEM((tiles, rows, HALO), jnp.float32),
             pltpu.VMEM((tiles, rows, HALO), jnp.float32),
+            pltpu.VMEM((rows, HALO), jnp.float32),
             pltpu.SemaphoreType.DMA((tiles,)),
             pltpu.SemaphoreType.DMA((SUB, 2)),
             pltpu.SemaphoreType.DMA((SUB, 2, rows // chunk)),
@@ -271,7 +295,15 @@
             pltpu.SemaphoreType.DMA,
         ],
         compiler_params=pltpu.CompilerParams(collective_id=0, has_side_effects=True),
-    )(field, columns, current, position)
+    )(
+        field,
+        wave_speed,
+        substeps,
+        jnp.asarray(trig),
+        east.reshape(1, width),
+        north.reshape(1, width),
+        neighbours,
+    )
 
 
 def source_kernel(batch, quad_ref, strength_ref, points_ref, blocks_ref, out_ref, rounded):
@@ -313,7 +345,7 @@
     vmem = pl.BlockSpec(memory_space=pltpu.VMEM)
     smem = pl.BlockSpec(memory_space=pltpu.SMEM)
     out = pl.pallas_call(
-        functools.partial(source_kernel, math.gcd(blocks.shape[0], 4)),
+        functools.partial(source_kernel, math.gcd(blocks.shape[0], 16)),
         out_shape=jax.ShapeDtypeStruct((NF, ND, width), jnp.float32),
         in_specs=[smem, smem, vmem, vmem],
         out_specs=vmem,
@@ -380,26 +412,9 @@
     spaces = lax.axis_size("space")
     rows, width = spectrum.shape
     assert width == peers * HALO
-    first = lax.axis_index("comp") * rows
-    angles = (np.arange(ND, dtype=np.float32) + np.float32(0.5)) * np.float32(2.0 * math.pi / ND)
-    counts = substeps.astype(jnp.float32)
-    columns = jnp.stack(
-        [
-            (wave_speed[:, None] * np.cos(angles)[None, :]).reshape(NF * ND),
-            (wave_speed[:, None] * np.sin(angles)[None, :]).reshape(NF * ND),
-            courant_scale / counts,
-            counts,
-        ],
-        axis=1,
+    points = propagate(
+        spectrum, wave_speed, substeps, current_east, current_north, neighbours, peers, spaces
     )
-    columns = lax.dynamic_slice_in_dim(columns, first, rows)
-    tiles = width // HALO
-    current = jnp.stack(
-        [current_east.reshape(tiles, HALO), current_north.reshape(tiles, HALO)], axis=1
-    )
-    position = neighbours.reshape(4, tiles, HALO) - HALO * jnp.arange(tiles)[None, :, None]
-    position = position.transpose(1, 0, 2)
-    points = propagate(spectrum, columns, current, position, peers, spaces)
     points = source_term(points, blocks, quad_index, strength)
     return send_home(points, peers)
 

time: 103 us -> 102 us (level)
  other arithmetic: 4.93 us -> 0 us
  Pallas kernels: 94.5 us -> 99.4 us
  local copies, waits for them, and re-layouts: 3.43 us -> 2.36 us
    pallas_call x1, Pallas kernels: 49.1 us -> 55 us  [propagate(): pl.pallas_call(functools.partial(propagate_kernel, peers, spaces, chunk),...]
    pallas_call x1, Pallas kernels: 14.1 us -> 12 us  [source_term(): pl.pallas_call(functools.partial(source_kernel, math.gcd(blocks.shape[0],...]
    another operation x2 -> x0, other arithmetic: 1.38 us -> none  [the longest x1 1.29 us: shards(): jnp.stack([current_east.reshape(tiles, HALO), current_north.reshape(tiles...]
    transpose x1 -> x0, other arithmetic: 1.36 us -> none  [shards(): position = position.transpose(1, 0, 2)]
    pallas_call x1, Pallas kernels: 31.2 us -> 32.3 us  [send_home(): pl.pallas_call(functools.partial(home_kernel, peers), out_shape=jax.Shape...]
    unnamed x2 -> x1, local copies, waits for them, and re-layouts: 3.25 us -> 2.36 us
where the time goes in v2:
time: 102 us
  Pallas kernels  99.4 us (97%)
  local copies, waits for them, and re-layouts  2.36 us (2%)
    pallas_call x1, Pallas kernels, propagate(): pl.pallas_call(functools.partial(propagate_kernel, peers, spaces, chunk),...  55 us
    pallas_call x1, Pallas kernels, send_home(): pl.pallas_call(functools.partial(home_kernel, peers), out_shape=jax.Shape...  32.3 us
    pallas_call x1, Pallas kernels, source_term(): pl.pallas_call(functools.partial(source_kernel, math.gcd(blocks.shape[0],...  12 us
    unnamed x1, local copies, waits for them, and re-layouts  2.36 us

profile of v2, /device:TPU:12, one launch (start us, length us, event | category | flops | bytes accessed | tf_op | source)
XLA Modules:
  0.0 101.8 jit_solution(3425182855792246006)
XLA Ops:
  0.0 55.0 %shard_map.100 = f32[2304,128]{1,0:T(8,128)} custom-call(f32[576,512]{1,0:T(8,128)} %field_ref.1, f32[36]{0:T(128)} %wave_ref.1, s32[2304]{0:T(1024)} %substeps_ref.1, f32[2,64,128]{2,1,0:T(8,128)} %constant.2.clone.trig_ref, f32[1,512]{1,0:T(1,128)} %bitcast.6, f32[1,512]{1,0:T(1,128)} %bitcast.7, s32[4,512]{1,0:T(4,128)} %neighbour_ref.1), custom_call_target="tpu_custom_call" | custom-call | tf_op jit(solution)/shard_map/pallas_call | solution.py:280
  55.1 12.0 %shard_map.101 = f32[36,64,128]{2,1,0:T(8,128)} custom-call(s32[4,64]{1,0:T(4,128)} %quad_ref.1, f32[64]{0:T(128)} %strength_ref.1, f32[36,64,128]{2,1,0:T(8,128)} %bitcast.4, bf16[64,64,64]{2,1,0:T(8,128)(2,1)} %blocks_ref.1), custom_call_target="tpu_custom_call" | custom-call | tf_op jit(solution)/shard_map/pallas_call | solution.py:347
  67.1 32.3 %shard_map.102 = f32[576,512]{1,0:T(8,128)} custom-call(f32[2304,128]{1,0:T(8,128)} %bitcast.5), custom_call_target="tpu_custom_call" | custom-call | tf_op jit(solution)/shard_map/pallas_call | solution.py:386
  99.5 2.4 %copy.12 = f32[576,512]{1,0:T(8,128)} copy(f32[576,512]{1,0:T(8,128)} %shard_map.102) | data formatting | bytes 2359296

commit v3 on v2

--- a/solution.py
+++ b/solution.py
@@ -13,7 +13,7 @@
 ND = 64
 SUB = 4
 HALO = 128
-SKEW = 1
+SKEW = 2
 
 courant_scale = 0.4
 courant_limit = 0.45
@@ -64,6 +64,7 @@
     speed_x,
     speed_y,
     repeats,
+    selector,
     load_sem,
     halo_send,
     halo_recv,
@@ -192,45 +193,58 @@
 
         lax.fori_loop(0, chunk // 8, per_group, 0)
 
+    def choices(j, carry):
+        spot = lax.broadcasted_iota(jnp.int32, (2 * HALO, HALO), 0)
+        for d in range(4):
+            wanted = neighbour_ref[d : d + 1, lanes(j)] - (j + d % 2) * HALO
+            chosen = jnp.where(spot == wanted, 1.0, 0.0).astype(jnp.bfloat16)
+            half = d // 2 * HALO
+            selector[j, d % 2, :, half : half + HALO] = chosen
+        return carry
+
+    def split(x):
+        high = x.astype(jnp.bfloat16)
+        rest = x - high.astype(jnp.float32)
+        middle = rest.astype(jnp.bfloat16)
+        low = (rest - middle.astype(jnp.float32)).astype(jnp.bfloat16)
+        return high, middle, low
+
+    def pick(first, second, chosen):
+        pairs = [jnp.concatenate(pair, axis=1) for pair in zip(first, second)]
+        if chunk % 16 == 0:
+            taken = jnp.dot(
+                jnp.concatenate(pairs, axis=0), chosen, preferred_element_type=jnp.float32
+            )
+            terms = [taken[i * chunk : (i + 1) * chunk] for i in range(3)]
+        else:
+            terms = [jnp.dot(p, chosen, preferred_element_type=jnp.float32) for p in pairs]
+        taken = terms[0] + terms[1] + terms[2]
+        return taken[:, :HALO], taken[:, HALO:]
+
     def advance(s, c):
+        at = pl.ds(c * chunk, chunk)
+
         def per_tile(j, carry):
-            west, east, south, north = [
-                jnp.broadcast_to(neighbour_ref[d : d + 1, lanes(j)] - j * HALO, (8, HALO))
-                for d in range(4)
-            ]
-
-            def upwind(speed, near, far, before, here_tile, after):
-                spot = jnp.where(speed > 0.0, near, far)
-                lane = spot & (HALO - 1)
-                taken = [
-                    jnp.take_along_axis(tile, lane, axis=1, mode="promise_in_bounds")
-                    for tile in (before, here_tile, after)
-                ]
-                value = jnp.where(
-                    spot < HALO, taken[0], jnp.where(spot < 2 * HALO, taken[1], taken[2])
-                )
-                return jnp.abs(speed) * (here_tile - value)
-
-            def per_group(g, inner):
-                at = pl.ds(pl.multiple_of(c * chunk + g * 8, 8), 8)
-                before = states[s, j, at]
-                value = states[s, j + 1, at]
-                after = states[s, j + 2, at]
-                change = upwind(speed_x[j, at], west, east, before, value, after)
-                change = change + upwind(speed_y[j, at], south, north, before, value, after)
-                if s > 0:
-                    change = jnp.where(repeats[at] > float(s), change, 0.0)
-                states[s + 1, j + 1, at] = value - change
-                return inner
-
-            return lax.fori_loop(0, chunk // 8, per_group, carry, unroll=True)
-
-        lax.fori_loop(0, tiles, per_tile, 0)
+            value = states[s, j + 1, at]
+            here_split = split(value)
+            west, south = pick(split(states[s, j, at]), here_split, selector[j, 0])
+            east, north = pick(here_split, split(states[s, j + 2, at]), selector[j, 1])
+            along_x = speed_x[j, at]
+            along_y = speed_y[j, at]
+            change = jnp.abs(along_x) * (value - jnp.where(along_x > 0.0, west, east))
+            change = change + jnp.abs(along_y) * (value - jnp.where(along_y > 0.0, south, north))
+            if s > 0:
+                change = jnp.where(repeats[at] > float(s), change, 0.0)
+            states[s + 1, j + 1, at] = value - change
+            return carry
+
+        lax.fori_loop(0, tiles, per_tile, 0, unroll=2)
 
     for load in loads:
         load.wait()
     for c in range(chunks):
         send_halo(0, c)
+    lax.fori_loop(0, tiles, choices, 0)
     for wave in range(chunks + SKEW * (SUB - 1)):
         for s in reversed(range(SUB)):
             c = wave - SKEW * s
@@ -287,6 +301,7 @@
             pltpu.VMEM((tiles, rows, HALO), jnp.float32),
             pltpu.VMEM((tiles, rows, HALO), jnp.float32),
             pltpu.VMEM((rows, HALO), jnp.float32),
+            pltpu.VMEM((tiles, 2, 2 * HALO, 2 * HALO), jnp.bfloat16),
             pltpu.SemaphoreType.DMA((tiles,)),
             pltpu.SemaphoreType.DMA((SUB, 2)),
             pltpu.SemaphoreType.DMA((SUB, 2, rows // chunk)),
@@ -306,7 +321,7 @@
     )
 
 
-def source_kernel(batch, quad_ref, strength_ref, points_ref, blocks_ref, out_ref, rounded):
+def source_kernel(batch, quad_ref, strength_ref, points_ref, blocks_ref, out_ref, rounded, products):
     total = blocks_ref.shape[0]
 
     def fill(f, carry):
@@ -318,7 +333,6 @@
     lax.fori_loop(0, NF, fill, 0, unroll=4)
 
     def step(i, carry):
-        parts = []
         for b in range(batch):
             j = i * batch + b
             block = blocks_ref[j]
@@ -329,8 +343,11 @@
                 (((0,), (0,)), ((), ())),
                 preferred_element_type=jnp.float32,
             )
-            product = (left * right * points_ref[quad_ref[2, j]]).astype(jnp.bfloat16)
-            part = jnp.dot(block, product, preferred_element_type=jnp.float32)
+            products[b] = (left * right * points_ref[quad_ref[2, j]]).astype(jnp.bfloat16)
+        parts = []
+        for b in range(batch):
+            j = i * batch + b
+            part = jnp.dot(blocks_ref[j], products[b], preferred_element_type=jnp.float32)
             parts.append(part * (strength_ref[j] * source_step))
         for b in range(batch):
             target = quad_ref[3, i * batch + b]
@@ -344,12 +361,16 @@
     width = points.shape[1]
     vmem = pl.BlockSpec(memory_space=pltpu.VMEM)
     smem = pl.BlockSpec(memory_space=pltpu.SMEM)
+    batch = math.gcd(blocks.shape[0], 16)
     out = pl.pallas_call(
-        functools.partial(source_kernel, math.gcd(blocks.shape[0], 16)),
+        functools.partial(source_kernel, batch),
         out_shape=jax.ShapeDtypeStruct((NF, ND, width), jnp.float32),
         in_specs=[smem, smem, vmem, vmem],
         out_specs=vmem,
-        scratch_shapes=[pltpu.VMEM((NF, ND, width), jnp.bfloat16)],
+        scratch_shapes=[
+            pltpu.VMEM((NF, ND, width), jnp.bfloat16),
+            pltpu.VMEM((batch, ND, width), jnp.bfloat16),
+        ],
     )(quad_index, strength, points.reshape(NF, ND, width), blocks)
     return out.reshape(NF * ND, width)
 

time: 102 us -> 83 us (0.81)
  Pallas kernels: 99.4 us -> 80.3 us
    pallas_call x1, Pallas kernels: 55 us -> 44.4 us  [propagate(): pl.pallas_call(functools.partial(propagate_kernel, peers, spaces, chunk),...]
    pallas_call x1, Pallas kernels: 12 us -> 4.71 us  [source_term(): pl.pallas_call(functools.partial(source_kernel, batch), out_shape=jax.Sha...]
    pallas_call x1, Pallas kernels: 32.3 us -> 31.2 us  [send_home(): pl.pallas_call(functools.partial(home_kernel, peers), out_shape=jax.Shape...]
where the time goes in v3:
time: 83 us; the launch traced here: 82.7 us
  Pallas kernels  80.3 us (97%)
  local copies, waits for them, and re-layouts  2.36 us (3%)
    pallas_call x1, Pallas kernels, propagate(): pl.pallas_call(functools.partial(propagate_kernel, peers, spaces, chunk),...  44.4 us
    pallas_call x1, Pallas kernels, send_home(): pl.pallas_call(functools.partial(home_kernel, peers), out_shape=jax.Shape...  31.2 us
    pallas_call x1, Pallas kernels, source_term(): pl.pallas_call(functools.partial(source_kernel, batch), out_shape=jax.Sha...  4.71 us
    unnamed x1, local copies, waits for them, and re-layouts  2.36 us

profile of v3, /device:TPU:12, one launch (start us, length us, event | category | flops | bytes accessed | tf_op | source)
XLA Modules:
  0.0 82.7 jit_solution(6060593879062067777)
XLA Ops:
  0.0 44.4 %shard_map.100 = f32[2304,128]{1,0:T(8,128)} custom-call(f32[576,512]{1,0:T(8,128)} %field_ref.1, f32[36]{0:T(128)} %wave_ref.1, s32[2304]{0:T(1024)} %substeps_ref.1, f32[2,64,128]{2,1,0:T(8,128)} %constant.2.clone.trig_ref, f32[1,512]{1,0:T(1,128)} %bitcast.6, f32[1,512]{1,0:T(1,128)} %bitcast.7, s32[4,512]{1,0:T(4,128)} %neighbour_ref.1), custom_call_target="tpu_custom_call" | custom-call | tf_op jit(solution)/shard_map/pallas_call | solution.py:294
  44.4 4.7 %shard_map.101 = f32[36,64,128]{2,1,0:T(8,128)} custom-call(s32[4,64]{1,0:T(4,128)} %quad_ref.1, f32[64]{0:T(128)} %strength_ref.1, f32[36,64,128]{2,1,0:T(8,128)} %bitcast.4, bf16[64,64,64]{2,1,0:T(8,128)(2,1)} %blocks_ref.1), custom_call_target="tpu_custom_call" | custom-call | tf_op jit(solution)/shard_map/pallas_call | solution.py:365
  49.2 31.2 %shard_map.102 = f32[576,512]{1,0:T(8,128)} custom-call(f32[2304,128]{1,0:T(8,128)} %bitcast.5), custom_call_target="tpu_custom_call" | custom-call | tf_op jit(solution)/shard_map/pallas_call | solution.py:407
  80.4 2.4 %copy.12 = f32[576,512]{1,0:T(8,128)} copy(f32[576,512]{1,0:T(8,128)} %shard_map.102) | data formatting | bytes 2359296

commit v4 on v3

--- a/solution.py
+++ b/solution.py
@@ -238,7 +238,7 @@
             states[s + 1, j + 1, at] = value - change
             return carry
 
-        lax.fori_loop(0, tiles, per_tile, 0, unroll=2)
+        lax.fori_loop(0, tiles, per_tile, 0, unroll=4)
 
     for load in loads:
         load.wait()
@@ -361,7 +361,7 @@
     width = points.shape[1]
     vmem = pl.BlockSpec(memory_space=pltpu.VMEM)
     smem = pl.BlockSpec(memory_space=pltpu.SMEM)
-    batch = math.gcd(blocks.shape[0], 16)
+    batch = math.gcd(blocks.shape[0], 32)
     out = pl.pallas_call(
         functools.partial(source_kernel, batch),
         out_shape=jax.ShapeDtypeStruct((NF, ND, width), jnp.float32),

time: 83 us -> 81 us (0.976)
  Pallas kernels: 80.3 us -> 78.3 us
    pallas_call x1, Pallas kernels: 44.4 us -> 43.1 us  [propagate(): pl.pallas_call(functools.partial(propagate_kernel, peers, spaces, chunk),...]
where the time goes in v4:
time: 81 us; the launch traced here: 80.7 us
  Pallas kernels  78.3 us (97%)
  local copies, waits for them, and re-layouts  2.36 us (3%)
    pallas_call x1, Pallas kernels, propagate(): pl.pallas_call(functools.partial(propagate_kernel, peers, spaces, chunk),...  43.1 us
    pallas_call x1, Pallas kernels, send_home(): pl.pallas_call(functools.partial(home_kernel, peers), out_shape=jax.Shape...  31.2 us
    pallas_call x1, Pallas kernels, source_term(): pl.pallas_call(functools.partial(source_kernel, batch), out_shape=jax.Sha...  4.06 us
    unnamed x1, local copies, waits for them, and re-layouts  2.36 us

profile of v4, /device:TPU:12, one launch (start us, length us, event | category | flops | bytes accessed | tf_op | source)
XLA Modules:
  0.0 80.7 jit_solution(1884047148277743549)
XLA Ops:
  0.0 43.1 %shard_map.100 = f32[2304,128]{1,0:T(8,128)} custom-call(f32[576,512]{1,0:T(8,128)} %field_ref.1, f32[36]{0:T(128)} %wave_ref.1, s32[2304]{0:T(1024)} %substeps_ref.1, f32[2,64,128]{2,1,0:T(8,128)} %constant.2.clone.trig_ref, f32[1,512]{1,0:T(1,128)} %bitcast.6, f32[1,512]{1,0:T(1,128)} %bitcast.7, s32[4,512]{1,0:T(4,128)} %neighbour_ref.1), custom_call_target="tpu_custom_call" | custom-call | tf_op jit(solution)/shard_map/pallas_call | solution.py:294
  43.1 4.1 %shard_map.101 = f32[36,64,128]{2,1,0:T(8,128)} custom-call(s32[4,64]{1,0:T(4,128)} %quad_ref.1, f32[64]{0:T(128)} %strength_ref.1, f32[36,64,128]{2,1,0:T(8,128)} %bitcast.4, bf16[64,64,64]{2,1,0:T(8,128)(2,1)} %blocks_ref.1), custom_call_target="tpu_custom_call" | custom-call | tf_op jit(solution)/shard_map/pallas_call | solution.py:365
  47.2 31.2 %shard_map.102 = f32[576,512]{1,0:T(8,128)} custom-call(f32[2304,128]{1,0:T(8,128)} %bitcast.5), custom_call_target="tpu_custom_call" | custom-call | tf_op jit(solution)/shard_map/pallas_call | solution.py:407
  78.3 2.4 %copy.12 = f32[576,512]{1,0:T(8,128)} copy(f32[576,512]{1,0:T(8,128)} %shard_map.102) | data formatting | bytes 2359296
